TPU v7x, 256 devices: a whole 4x4x8 slice. The times are simulated.
256 devices in a mesh: seq: 64 (over z, y, core), head: 4 (over x).
Axes of the slice: x: 4, y: 4, z: 8, core: 2. Of those that a mesh axis runs over, the one named last changes fastest.
Arguments:
- rotated_query_rows: bfloat16 [32768, 4096], P(('seq', 'head')), may hold values from -8 to 8
- rotated_key_rows: bfloat16 [32768, 2048], P(('seq', 'head')), may hold values from -8 to 8
- value_matrix: bfloat16 [32768, 2048], P(('seq', 'head')), may hold values from -6 to 6
- output_gradient: bfloat16 [32768, 4096], P(('seq', 'head')), may hold values from -6 to 6
- doc_lengths: int32 [64], replicated, may hold values from 1 to 2048, 32768 in all
Outputs:
- attended: bfloat16 [32768, 4096], P(('seq', 'head'))
- query_grad: bfloat16 [32768, 4096], P(('seq', 'head'))
- key_gradient: bfloat16 [32768, 2048], P(('seq', 'head'))
- value_gradient: bfloat16 [32768, 2048], P(('seq', 'head'))
Inputs may be any that keep to these rules, and one draw needn't show every extreme that they name: `doc_lengths`: the lengths of the 64 documents packed in order; they sum to 32768 and the longest has 2048 tokens.
All inputs are finite; a program needn't handle non-finite values.
Results may differ from a plain program's by a relative error of at most 0.02.
Values may be sent and summed in bfloat16 or wider, within the bound.
A program may use at most 128 MiB of HBM per device.

v0:
```python
import jax
import jax.numpy as jnp
from jax import lax
from jax.sharding import PartitionSpec as P

HEAD_WIDTH = 256
WINDOW_LENGTH = 1024


query_tile = 512


def passed_along(block, axis, distance):
    devices = range(lax.axis_size(axis))
    route = [(i - distance, i) for i in devices if i - distance in devices]
    return lax.ppermute(block, axis, route)


def doc_index(positions, doc_lengths):
    starts = jnp.cumsum(doc_lengths) - doc_lengths
    counted = jnp.sum((starts[None, :] <= positions[:, None]).astype(jnp.int32), axis=1)
    return counted - 1


def tile_pass(
    query_block, grad_block, key_block, value_block, query_docs, query_place, key_docs, key_place
):
    score_scale = HEAD_WIDTH ** (-0.5)
    scores = (
        jnp.einsum("qgd,kd->gqk", query_block, key_block, preferred_element_type=jnp.float32)
        * score_scale
    )
    offsets = query_place[:, None] - key_place[None, :]
    visible = (
        (query_docs[:, None] == key_docs[None, :]) & (offsets >= 0) & (offsets < WINDOW_LENGTH)
    )
    scores = jnp.where(visible[None], scores, -jnp.inf)
    row_max = jnp.max(scores, axis=2, keepdims=True)
    weights = jnp.exp(scores - row_max)
    probs_full = weights / jnp.sum(weights, axis=2, keepdims=True)
    probs_low = probs_full.astype(jnp.bfloat16)
    attended = jnp.einsum(
        "gqk,kd->qgd", probs_low, value_block, preferred_element_type=jnp.float32
    ).astype(jnp.bfloat16)
    row_delta = jnp.sum(grad_block.astype(jnp.float32) * attended.astype(jnp.float32), axis=2)
    value_part = jnp.einsum(
        "gqk,qgd->kd", probs_low, grad_block, preferred_element_type=jnp.float32
    )
    grad_probs = jnp.einsum(
        "qgd,kd->gqk", grad_block, value_block, preferred_element_type=jnp.float32
    )
    grad_low = (probs_full * (grad_probs - jnp.transpose(row_delta)[:, :, None])).astype(
        jnp.bfloat16
    )
    query_grad = (
        jnp.einsum("gqk,kd->qgd", grad_low, key_block, preferred_element_type=jnp.float32)
        * score_scale
    ).astype(jnp.bfloat16)
    key_part = (
        jnp.einsum("gqk,qgd->kd", grad_low, query_block, preferred_element_type=jnp.float32)
        * score_scale
    )
    return (attended, query_grad, key_part, value_part)


def head_sweep(query_head, grad_head, kv_head, key_docs, key_place, own_start):
    block_rows = query_head.shape[0]
    tile_rows = min(block_rows, query_tile)
    finish = own_start + tile_rows
    key_start = finish - tile_rows - WINDOW_LENGTH
    results = tile_pass(
        query_head,
        grad_head,
        kv_head[0, key_start:finish],
        kv_head[1, key_start:finish],
        key_docs[own_start:finish],
        key_place[own_start:finish],
        key_docs,
        key_place,
    )
    attended_tiles = results[0]
    grad_tiles = results[1]
    key_gradient_sums = results[2]
    value_gradient_sums = results[3]
    return (attended_tiles, grad_tiles, key_gradient_sums, value_gradient_sums)


def attend(exchanged, doc_lengths, group_width):
    query_parts, key_parts, value_parts, grad_parts = exchanged
    block_rows = query_parts.shape[0]
    head_items = query_parts.shape[2]
    kv_block = jnp.stack([key_parts[:, 0], value_parts[:, 0]], axis=0)
    rim_count = (WINDOW_LENGTH + block_rows - 2) // block_rows
    margin = max(0, WINDOW_LENGTH - rim_count * block_rows)
    rim_blocks = [passed_along(kv_block, "seq", distance) for distance in range(1, rim_count + 1)]
    pieces = (
        [jnp.zeros((2, margin, head_items, HEAD_WIDTH), jnp.bfloat16)]
        + rim_blocks[::-1]
        + [kv_block]
    )
    kv_window = jnp.concatenate(pieces, axis=1)
    own_start = margin + rim_count * block_rows
    key_length = own_start + block_rows
    key_place = (
        lax.axis_index("seq") * block_rows - own_start + jnp.arange(key_length, dtype=jnp.int32)
    )
    key_docs = doc_index(key_place, doc_lengths)
    outputs = []
    for head_item in range(head_items):
        query_head = query_parts[:, 0, head_item].reshape(block_rows, group_width, HEAD_WIDTH)
        grad_head = grad_parts[:, 0, head_item].reshape(block_rows, group_width, HEAD_WIDTH)
        kv_head = kv_window[:, :, head_item]
        swept_head = head_sweep(query_head, grad_head, kv_head, key_docs, key_place, own_start)
        outputs.append(swept_head)
    attended = jnp.stack([swept_head[0] for swept_head in outputs], axis=1).reshape(
        block_rows, 1, head_items, group_width * HEAD_WIDTH
    )
    query_grad = jnp.stack([swept_head[1] for swept_head in outputs], axis=1).reshape(
        block_rows, 1, head_items, group_width * HEAD_WIDTH
    )
    partial_grads = jnp.stack(
        [jnp.stack([swept_head[2], swept_head[3]], axis=0) for swept_head in outputs], axis=2
    )
    own_part = partial_grads[:, own_start:]
    gathered = own_part
    for distance in range(1, rim_count + 1):
        gathered = gathered + passed_along(
            partial_grads[
                :, own_start - distance * block_rows : own_start - (distance - 1) * block_rows
            ],
            "seq",
            -distance,
        )
    key_gradient = gathered[0].astype(jnp.bfloat16)[:, None]
    value_gradient = gathered[1].astype(jnp.bfloat16)[:, None]
    return (
        lax.all_to_all(attended, "head", split_axis=0, concat_axis=1, tiled=True),
        lax.all_to_all(query_grad, "head", split_axis=0, concat_axis=1, tiled=True),
        lax.all_to_all(key_gradient, "head", split_axis=0, concat_axis=1, tiled=True),
        lax.all_to_all(value_gradient, "head", split_axis=0, concat_axis=1, tiled=True),
    )


def shards(rotated_query_rows, rotated_key_rows, value_matrix, output_gradient, doc_lengths):
    token_total = rotated_query_rows.shape[0]
    groups_count = lax.axis_size("head")
    kv_count = rotated_key_rows.shape[1] // HEAD_WIDTH
    per_device = kv_count // groups_count
    group_width = rotated_query_rows.shape[1] // rotated_key_rows.shape[1]
    query_split = rotated_query_rows.reshape(
        token_total, groups_count, per_device, group_width * HEAD_WIDTH
    )
    key_split = rotated_key_rows.reshape(token_total, groups_count, per_device, HEAD_WIDTH)
    value_split = value_matrix.reshape(token_total, groups_count, per_device, HEAD_WIDTH)
    grad_split = output_gradient.reshape(
        token_total, groups_count, per_device, group_width * HEAD_WIDTH
    )
    attended, query_grad, key_gradient, value_gradient = attend(
        (
            lax.all_to_all(query_split, "head", split_axis=1, concat_axis=0, tiled=True),
            lax.all_to_all(key_split, "head", split_axis=1, concat_axis=0, tiled=True),
            lax.all_to_all(value_split, "head", split_axis=1, concat_axis=0, tiled=True),
            lax.all_to_all(grad_split, "head", split_axis=1, concat_axis=0, tiled=True),
        ),
        doc_lengths,
        group_width,
    )
    return (
        attended.reshape(token_total, rotated_query_rows.shape[1]),
        query_grad.reshape(token_total, rotated_query_rows.shape[1]),
        key_gradient.reshape(token_total, rotated_key_rows.shape[1]),
        value_gradient.reshape(token_total, rotated_key_rows.shape[1]),
    )


def solution(mesh):
    in_specs = (
        P(("seq", "head"), None),
        P(("seq", "head"), None),
        P(("seq", "head"), None),
        P(("seq", "head"), None),
        P(),
    )
    out_specs = (
        P(("seq", "head"), None),
        P(("seq", "head"), None),
        P(("seq", "head"), None),
        P(("seq", "head"), None),
    )
    return jax.shard_map(shards, mesh=mesh, in_specs=in_specs, out_specs=out_specs, check_vma=False)
```

profile of v0, /device:TPU:122, one launch (start us, length us, event | category | flops | bytes accessed | tf_op | source)
XLA Modules:
  0.0 237.3 jit_solution(12690508888914768315)
XLA Ops:
  3.1 4.8 %all-to-all-start = ((bf16[128,4,2,256]{3,0,2,1:T(8,128)(2,1)}), bf16[128,4,2,256]{3,0,2,1:T(8,128)(2,1)S(1)}, u32[]{:S(2)}, u32[]{:S(2)}) async-start(bf16[128,4,2,256]{3,0,2,1:T(8,128)(2,1)} %copy.160), calls=%async_computation | async-start | bytes 1048576 | tf_op jit(solution)/shard_map/all_to_all | solution.py:161
  9.2 6.7 %all-to-all-done = bf16[128,4,2,256]{3,0,2,1:T(8,128)(2,1)S(1)} async-done(((bf16[128,4,2,256]{3,0,2,1:T(8,128)(2,1)}), bf16[128,4,2,256]{3,0,2,1:T(8,128)(2,1)S(1)}, u32[]{:S(2)}, u32[]{:S(2)}) %all-to-all-start) | async-done | bytes 524320 | tf_op jit(solution)/shard_map/all_to_all | solution.py:161
  15.9 4.9 %all-to-all-start.1 = ((bf16[128,4,2,256]{3,0,2,1:T(8,128)(2,1)}), bf16[128,4,2,256]{3,0,2,1:T(8,128)(2,1)S(1)}, u32[]{:S(2)}, u32[]{:S(2)}) async-start(bf16[128,4,2,256]{3,0,2,1:T(8,128)(2,1)} %copy.163), calls=%async_computation.1 | async-start | bytes 1048576 | tf_op jit(solution)/shard_map/all_to_all | solution.py:162
  22.1 5.5 %all-to-all-done.1 = bf16[128,4,2,256]{3,0,2,1:T(8,128)(2,1)S(1)} async-done(((bf16[128,4,2,256]{3,0,2,1:T(8,128)(2,1)}), bf16[128,4,2,256]{3,0,2,1:T(8,128)(2,1)S(1)}, u32[]{:S(2)}, u32[]{:S(2)}) %all-to-all-start.1) | async-done | bytes 524320 | tf_op jit(solution)/shard_map/all_to_all | solution.py:162
  27.7 4.9 %all-to-all-start.2 = ((bf16[128,4,2,512]{0,3,2,1:T(8,128)(2,1)}), bf16[128,4,2,512]{0,3,2,1:T(8,128)(2,1)S(1)}, u32[]{:S(2)}, u32[]{:S(2)}) async-start(bf16[128,4,2,512]{0,3,2,1:T(8,128)(2,1)} %bitcast.13), calls=%async_computation.2 | async-start | bytes 2097152 | tf_op jit(solution)/shard_map/all_to_all | solution.py:160
  38.1 5.7 %all-to-all-done.2 = bf16[128,4,2,512]{0,3,2,1:T(8,128)(2,1)S(1)} async-done(((bf16[128,4,2,512]{0,3,2,1:T(8,128)(2,1)}), bf16[128,4,2,512]{0,3,2,1:T(8,128)(2,1)S(1)}, u32[]{:S(2)}, u32[]{:S(2)}) %all-to-all-start.2) | async-done | bytes 1048608 | tf_op jit(solution)/shard_map/all_to_all | solution.py:160
  43.8 5.1 %all-to-all-start.4 = ((bf16[128,4,2,512]{3,2,0,1:T(2,128)(2,1)}), bf16[128,4,2,512]{3,2,0,1:T(2,128)(2,1)S(1)}, u32[]{:S(2)}, u32[]{:S(2)}) async-start(bf16[128,4,2,512]{3,2,0,1:T(2,128)(2,1)} %copy.180), calls=%async_computation.4 | async-start | bytes 2097152 | tf_op jit(solution)/shard_map/all_to_all | solution.py:163
  51.9 4.7 %collective-permute-start = (bf16[2,512,2,256]{3,1,2,0:T(8,128)(2,1)}, bf16[2,512,2,256]{3,1,2,0:T(8,128)(2,1)}, u32[]{:S(2)}, u32[]{:S(2)}) collective-permute-start(bf16[2,512,2,256]{3,1,2,0:T(8,128)(2,1)} %pad_maximum_fusion.1), channel_id=1, source_target_pairs={{0,8},{4,12},{8,16},{12,20},{16,24},{20,28},{24,32},{28,36},{32,40... | collective-permute-start | bytes 3145736 | tf_op jit(solution)/shard_map/ppermute | solution.py:16
  69.4 5.7 %collective-permute-done.1 = bf16[2,512,2,256]{3,1,2,0:T(8,128)(2,1)} collective-permute-done((bf16[2,512,2,256]{3,1,2,0:T(8,128)(2,1)}, bf16[2,512,2,256]{3,1,2,0:T(8,128)(2,1)}, u32[]{:S(2)}, u32[]{:S(2)}) %collective-permute-start.1) | collective-permute-done | bytes 1048608 | tf_op jit(solution)/shard_map/ppermute | solution.py:16
  75.1 5.4 %collective-permute-done = bf16[2,512,2,256]{3,1,2,0:T(8,128)(2,1)} collective-permute-done((bf16[2,512,2,256]{3,1,2,0:T(8,128)(2,1)}, bf16[2,512,2,256]{3,1,2,0:T(8,128)(2,1)}, u32[]{:S(2)}, u32[]{:S(2)}) %collective-permute-start) | collective-permute-done | bytes 1048608 | tf_op jit(solution)/shard_map/ppermute | solution.py:16
  82.7 7.3 %fusion.42 = (f32[2,512]{1,0:T(2,128)S(1)}, f32[2,512,1536]{1,2,0:T(8,128)}) fusion(pred[512,1536]{0,1:T(8,128)(4,1)} %fusion.13, bf16[512,2,256]{0,2,1:T(8,128)(2,1)} %bitcast.208, bf16[2,1536,2,256]{3,1,2,0:T(8,128)(2,1)S(1)} %maximum_maximum_fusion), kind=kOutput, calls=%fused_computation.80 | convolution fusion | flops 811599360 | bytes 8392704 | tf_op jit(solution)/shard_map/sub | solution.py:39
  90.0 3.7 %fusion.20 = bf16[2,512,1536]{1,2,0:T(8,128)(2,1)S(1)} fusion(f32[2,512,1536]{1,2,0:T(8,128)} %get-tuple-element.15, f32[2,512]{1,0:T(2,128)S(1)} %get-tuple-element.14), kind=kLoop, calls=%fused_computation.41 | loop fusion | flops 3145728 | bytes 9441280 | tf_op jit(solution)/shard_map/convert_element_type | solution.py:41
  97.7 6.3 %fusion.41 = (f32[2,512]{1,0:T(2,128)S(1)}, f32[2,512,1536]{1,2,0:T(8,128)}) fusion(pred[512,1536]{0,1:T(8,128)(4,1)} %fusion.13, bf16[512,2,256]{0,2,1:T(8,128)(2,1)} %bitcast.206, bf16[2,1536,2,256]{3,1,2,0:T(8,128)(2,1)S(1)} %maximum_maximum_fusion), kind=kOutput, calls=%fused_computation.79 | convolution fusion | flops 811599360 | bytes 8392704 | tf_op jit(solution)/shard_map/sub | solution.py:39
  104.0 3.8 %fusion.21 = bf16[2,512,1536]{1,2,0:T(8,128)(2,1)S(1)} fusion(f32[2,512,1536]{1,2,0:T(8,128)} %get-tuple-element.13, f32[2,512]{1,0:T(2,128)S(1)} %get-tuple-element.12), kind=kLoop, calls=%fused_computation.42 | loop fusion | flops 3145728 | bytes 9441280 | tf_op jit(solution)/shard_map/convert_element_type | solution.py:41
  118.6 2.7 %fusion.22 = (f32[2,512,2,256]{3,1,0,2:T(8,128)}, f32[2,512,2,256]{3,1,0,2:T(8,128)}) fusion(f32[2,1536,1,256]{3,1,0,2:T(8,128)S(1)} %get-tuple-element.20, f32[2,1536,1,256]{3,1,0,2:T(8,128)S(1)} %get-tuple-element.21), kind=kLoop, calls=%fused_computation.43 | loop fusion | flops 1048576 | bytes 10485760 | tf_op jit(solution)/shard_map/stack | solution.py:121
  121.6 10.4 %collective-permute-start.2 = (f32[2,512,2,256]{3,1,0,2:T(8,128)}, f32[2,512,2,256]{3,1,0,2:T(8,128)}, u32[]{:S(2)}, u32[]{:S(2)}) collective-permute-start(f32[2,512,2,256]{3,1,0,2:T(8,128)} %get-tuple-element.4), channel_id=1, source_target_pairs={{4,0},{8,4},{12,8},{16,12},{20,16},{24,20},{28,24},{32,28},{36,32}... | collective-permute-start | bytes 6291464 | tf_op jit(solution)/shard_map/ppermute | solution.py:16
  132.0 2.4 collective-permute-start.3
  134.4 3.6 %copy.176 = bf16[512,1,1,512]{3,2,1,0:T(2,128)(2,1)} copy(bf16[512,1,1,512]{0,3,2,1:T(8,128)(2,1)} %bitcast.198) | data formatting | bytes 1048576 | tf_op jit(solution)/shard_map/stack | solution.py:115
  137.9 3.6 %copy.177 = bf16[512,1,1,512]{3,2,1,0:T(2,128)(2,1)} copy(bf16[512,1,1,512]{0,3,2,1:T(8,128)(2,1)} %bitcast.202) | data formatting | bytes 1048576 | tf_op jit(solution)/shard_map/stack | solution.py:115
  141.5 4.2 %pad_maximum_fusion.2 = bf16[512,1,2,512]{3,2,1,0:T(2,128)(2,1)} fusion(bf16[512,1,1,512]{3,2,1,0:T(2,128)(2,1)} %copy.177, bf16[512,1,1,512]{3,2,1,0:T(2,128)(2,1)} %copy.176), kind=kLoop, calls=%fused_computation.56 | loop fusion | flops 2097152 | bytes 2097152 | tf_op jit(solution)/shard_map/stack | solution.py:115
  145.7 4.8 %all-to-all-start.3 = ((bf16[512,1,2,512]{3,2,1,0:T(2,128)(2,1)}), bf16[512,1,2,512]{3,2,1,0:T(2,128)(2,1)}, u32[]{:S(2)}, u32[]{:S(2)}) async-start(bf16[512,1,2,512]{3,2,1,0:T(2,128)(2,1)} %pad_maximum_fusion.2), calls=%async_computation.3 | async-start | bytes 2097152 | tf_op jit(solution)/shard_map/all_to_all | solution.py:137
  150.5 3.9 %fusion.27 = bf16[256,2,512]{2,0,1:T(8,128)(2,1)} fusion(bf16[2,512,1536]{1,2,0:T(8,128)(2,1)} %copy-done.4, bf16[2,1536,2,256]{3,1,2,0:T(8,128)(2,1)} %copy-done.1), kind=kOutput, calls=%fused_computation.51 | convolution fusion | flops 805830656 | bytes 4456448 | tf_op jit(solution)/shard_map/gqk,kd->qgd/dot_general | solution.py:56
  154.4 3.6 %copy.189 = bf16[512,1,1,512]{3,2,1,0:T(2,128)(2,1)} copy(bf16[512,1,1,512]{0,3,2,1:T(8,128)(2,1)} %bitcast.191) | data formatting | bytes 1048576 | tf_op jit(solution)/shard_map/stack | solution.py:118
  158.0 3.9 %fusion.28 = bf16[256,2,512]{2,0,1:T(8,128)(2,1)} fusion(bf16[2,512,1536]{1,2,0:T(8,128)(2,1)} %copy-done.5, bf16[2,1536,2,256]{3,1,2,0:T(8,128)(2,1)} %copy-done.1), kind=kOutput, calls=%fused_computation.52 | convolution fusion | flops 805830656 | bytes 4456448 | tf_op jit(solution)/shard_map/gqk,kd->qgd/dot_general | solution.py:56
  161.9 3.6 %copy.190 = bf16[512,1,1,512]{3,2,1,0:T(2,128)(2,1)} copy(bf16[512,1,1,512]{0,3,2,1:T(8,128)(2,1)} %bitcast.190) | data formatting | bytes 1048576 | tf_op jit(solution)/shard_map/stack | solution.py:118
  165.5 4.2 %pad_maximum_fusion.3 = bf16[512,1,2,512]{3,2,1,0:T(2,128)(2,1)} fusion(bf16[512,1,1,512]{3,2,1,0:T(2,128)(2,1)} %copy.190, bf16[512,1,1,512]{3,2,1,0:T(2,128)(2,1)} %copy.189), kind=kLoop, calls=%fused_computation.57 | loop fusion | flops 2097152 | bytes 2097152 | tf_op jit(solution)/shard_map/stack | solution.py:118
  169.7 4.8 %all-to-all-start.5 = ((bf16[512,1,2,512]{3,2,1,0:T(2,128)(2,1)}), bf16[512,1,2,512]{3,2,1,0:T(2,128)(2,1)}, u32[]{:S(2)}, u32[]{:S(2)}) async-start(bf16[512,1,2,512]{3,2,1,0:T(2,128)(2,1)} %pad_maximum_fusion.3), calls=%async_computation.5 | async-start | bytes 2097152 | tf_op jit(solution)/shard_map/all_to_all | solution.py:138
  176.7 29.7 %collective-permute-done.3 = f32[2,512,2,256]{3,1,0,2:T(8,128)} collective-permute-done((f32[2,512,2,256]{3,1,0,2:T(8,128)}, f32[2,512,2,256]{3,1,0,2:T(8,128)}, u32[]{:S(2)}, u32[]{:S(2)}) %collective-permute-start.3) | collective-permute-done | bytes 2097184 | tf_op jit(solution)/shard_map/ppermute | solution.py:16
  206.4 2.8 %fusion.26 = bf16[2,512,2,256]{3,1,0,2:T(8,128)(2,1)S(1)} fusion(f32[2,512,2,256]{3,1,0,2:T(8,128)} %collective-permute-done.3, f32[2,512,2,256]{3,1,0,2:T(8,128)} %collective-permute-done.2, f32[2,1536,1,256]{3,1,0,2:T(8,128)S(1)} %get-tuple-element.20, f32[2,1536,1,256]{3,1,0,2:T(8,128)} %copy-done), kind=kLoop, calls=%fused_computation.47 | loop fusion | flops 2097152 | bytes 11534336 | tf_op jit(solution)/shard_map/convert.1
  210.7 4.8 %all-to-all-start.7 = ((bf16[512,1,2,256]{3,2,1,0:T(2,128)(2,1)}), bf16[512,1,2,256]{3,2,1,0:T(2,128)(2,1)S(1)}, u32[]{:S(2)}, u32[]{:S(2)}) async-start(bf16[512,1,2,256]{3,2,1,0:T(2,128)(2,1)} %copy.198), calls=%async_computation.7 | async-start | bytes 1048576 | tf_op jit(solution)/shard_map/all_to_all | solution.py:140
  216.8 5.3 %all-to-all-done.7 = bf16[512,1,2,256]{3,2,1,0:T(2,128)(2,1)S(1)} async-done(((bf16[512,1,2,256]{3,2,1,0:T(2,128)(2,1)}), bf16[512,1,2,256]{3,2,1,0:T(2,128)(2,1)S(1)}, u32[]{:S(2)}, u32[]{:S(2)}) %all-to-all-start.7) | async-done | bytes 524320 | tf_op jit(solution)/shard_map/all_to_all | solution.py:140
  222.1 4.9 %all-to-all-start.6 = ((bf16[512,1,2,256]{3,2,1,0:T(2,128)(2,1)}), bf16[512,1,2,256]{3,2,1,0:T(2,128)(2,1)S(1)}, u32[]{:S(2)}, u32[]{:S(2)}) async-start(bf16[512,1,2,256]{3,2,1,0:T(2,128)(2,1)} %copy.196), calls=%async_computation.6 | async-start | bytes 1048576 | tf_op jit(solution)/shard_map/all_to_all | solution.py:139
  (106 shorter events, 58.3 us)
Async XLA Ops:
  0.6 7.3 %copy-start.12 = (bf16[128,2048]{1,0:T(8,128)(2,1)S(1)}, bf16[128,2048]{1,0:T(8,128)(2,1)}, u32[]{:S(2)}) copy-start(bf16[128,2048]{1,0:T(8,128)(2,1)} %param.7) | copy-start | bytes 1572868
  0.6 20.2 %copy-start.11 = (bf16[128,4096]{1,0:T(8,128)(2,1)S(1)}, bf16[128,4096]{1,0:T(8,128)(2,1)}, u32[]{:S(2)}) copy-start(bf16[128,4096]{1,0:T(8,128)(2,1)} %param.5) | copy-start | bytes 3145732
  3.1 12.8 %all-to-all-start = ((bf16[128,4,2,256]{3,0,2,1:T(8,128)(2,1)}), bf16[128,4,2,256]{3,0,2,1:T(8,128)(2,1)S(1)}, u32[]{:S(2)}, u32[]{:S(2)}) async-start(bf16[128,4,2,256]{3,0,2,1:T(8,128)(2,1)} %copy.160), calls=%async_computation | async-start | bytes 1048576 | tf_op jit(solution)/shard_map/all_to_all | solution.py:161
  8.2 24.4 %copy-start.19 = (s32[64]{0:T(128)S(1)}, s32[64]{0:T(128)}, u32[]{:S(2)}) copy-start(s32[64]{0:T(128)} %param.9) | copy-start | bytes 772
  15.9 11.7 %all-to-all-start.1 = ((bf16[128,4,2,256]{3,0,2,1:T(8,128)(2,1)}), bf16[128,4,2,256]{3,0,2,1:T(8,128)(2,1)S(1)}, u32[]{:S(2)}, u32[]{:S(2)}) async-start(bf16[128,4,2,256]{3,0,2,1:T(8,128)(2,1)} %copy.163), calls=%async_computation.1 | async-start | bytes 1048576 | tf_op jit(solution)/shard_map/all_to_all | solution.py:162
  27.7 5.4 %copy-start.6 = (bf16[128,4,2,256]{3,0,2,1:T(8,128)(2,1)}, bf16[128,4,2,256]{3,0,2,1:T(8,128)(2,1)S(1)}, u32[]{:S(2)}) copy-start(bf16[128,4,2,256]{3,0,2,1:T(8,128)(2,1)S(1)} %all-to-all-done.1) | copy-start | bytes 1572868
  27.7 16.2 %all-to-all-start.2 = ((bf16[128,4,2,512]{0,3,2,1:T(8,128)(2,1)}), bf16[128,4,2,512]{0,3,2,1:T(8,128)(2,1)S(1)}, u32[]{:S(2)}, u32[]{:S(2)}) async-start(bf16[128,4,2,512]{0,3,2,1:T(8,128)(2,1)} %bitcast.13), calls=%async_computation.2 | async-start | bytes 2097152 | tf_op jit(solution)/shard_map/all_to_all | solution.py:160
  32.6 5.4 %copy-start.15 = (s32[1536]{0:T(1024)}, s32[1536]{0:T(1024)S(1)}, u32[]{:S(2)}) copy-start(s32[1536]{0:T(1024)S(1)} %iota_add_fusion) | copy-start | bytes 18436
  33.1 5.0 %copy-start.17 = (s32[1536]{0:T(1024)}, s32[1536]{0:T(1024)S(1)}, u32[]{:S(2)}) copy-start(s32[1536]{0:T(1024)S(1)} %broadcast_add_fusion) | copy-start | bytes 18436
  36.8 23.3 %copy-start.2 = (bf16[4,128,1,2,256]{4,1,0,3,2:T(8,128)(2,1)}, bf16[4,128,1,2,256]{4,1,0,3,2:T(8,128)(2,1)S(1)}, u32[]{:S(2)}) copy-start(bf16[4,128,1,2,256]{4,1,0,3,2:T(8,128)(2,1)S(1)} %copy.161) | copy-start | bytes 1572868
  38.1 22.0 %copy-start.3 = (bf16[4,128,1,2,256]{4,1,0,3,2:T(8,128)(2,1)}, bf16[4,128,1,2,256]{4,1,0,3,2:T(8,128)(2,1)S(1)}, u32[]{:S(2)}) copy-start(bf16[4,128,1,2,256]{4,1,0,3,2:T(8,128)(2,1)S(1)} %copy.164) | copy-start | bytes 1572868
  43.8 12.8 %copy-start.16 = (s32[1536]{0:T(1024)S(1)}, s32[1536]{0:T(1024)}, u32[]{:S(2)}) copy-start(s32[1536]{0:T(1024)} %copy-done.15) | copy-start | bytes 18436
  43.8 12.8 %slice-start.4 = ((s32[1536]{0:T(1024)}), s32[512]{0:T(512)S(1)}, s32[]{:S(2)}) async-start(s32[1536]{0:T(1024)} %copy-done.15), calls=%async_computation.12 | async-start | bytes 4096 | tf_op jit(solution)/shard_map/slice | solution.py:77
  43.8 12.8 %copy-start.18 = (s32[1536]{0:T(1024)S(1)}, s32[1536]{0:T(1024)}, u32[]{:S(2)}) copy-start(s32[1536]{0:T(1024)} %copy-done.17) | copy-start | bytes 18436
  43.8 12.8 %slice-start.5 = ((s32[1536]{0:T(1024)}), s32[512]{0:T(512)S(1)}, s32[]{:S(2)}) async-start(s32[1536]{0:T(1024)} %copy-done.17), calls=%async_computation.13 | async-start | bytes 4096 | tf_op jit(solution)/shard_map/slice | solution.py:76
  43.8 19.5 %all-to-all-start.4 = ((bf16[128,4,2,512]{3,2,0,1:T(2,128)(2,1)}), bf16[128,4,2,512]{3,2,0,1:T(2,128)(2,1)S(1)}, u32[]{:S(2)}, u32[]{:S(2)}) async-start(bf16[128,4,2,512]{3,2,0,1:T(2,128)(2,1)} %copy.180), calls=%async_computation.4 | async-start | bytes 2097152 | tf_op jit(solution)/shard_map/all_to_all | solution.py:163
  50.0 25.1 %collective-permute-start.1 = (bf16[2,512,2,256]{3,1,2,0:T(8,128)(2,1)}, bf16[2,512,2,256]{3,1,2,0:T(8,128)(2,1)}, u32[]{:S(2)}, u32[]{:S(2)}) collective-permute-start(bf16[2,512,2,256]{3,1,2,0:T(8,128)(2,1)} %pad_maximum_fusion.1), channel_id=1, source_target_pairs={{0,4},{4,8},{8,12},{12,16},{16,20},{20,24},{24,28},{28,32},{32,36}... | collective-permute-start | bytes 3145736 | tf_op jit(solution)/shard_map/ppermute | solution.py:16
  51.9 28.6 %collective-permute-start = (bf16[2,512,2,256]{3,1,2,0:T(8,128)(2,1)}, bf16[2,512,2,256]{3,1,2,0:T(8,128)(2,1)}, u32[]{:S(2)}, u32[]{:S(2)}) collective-permute-start(bf16[2,512,2,256]{3,1,2,0:T(8,128)(2,1)} %pad_maximum_fusion.1), channel_id=1, source_target_pairs={{0,8},{4,12},{8,16},{12,20},{16,24},{20,28},{24,32},{28,36},{32,40... | collective-permute-start | bytes 3145736 | tf_op jit(solution)/shard_map/ppermute | solution.py:16
  82.7 31.1 %copy-start.1 = (bf16[2,1536,2,256]{3,1,2,0:T(8,128)(2,1)}, bf16[2,1536,2,256]{3,1,2,0:T(8,128)(2,1)S(1)}, u32[]{:S(2)}) copy-start(bf16[2,1536,2,256]{3,1,2,0:T(8,128)(2,1)S(1)} %maximum_maximum_fusion) | copy-start | bytes 9437188
  90.0 3.7 %copy-start.8 = (bf16[512,1,1,512]{0,3,2,1:T(8,128)(2,1)S(1)}, bf16[512,1,1,512]{0,3,2,1:T(8,128)(2,1)}, u32[]{:S(2)}) copy-start(bf16[512,1,1,512]{0,3,2,1:T(8,128)(2,1)} %copy.220) | copy-start | bytes 1572868
  104.0 3.9 %copy-start.7 = (bf16[512,1,1,512]{0,3,2,1:T(8,128)(2,1)S(1)}, bf16[512,1,1,512]{0,3,2,1:T(8,128)(2,1)}, u32[]{:S(2)}) copy-start(bf16[512,1,1,512]{0,3,2,1:T(8,128)(2,1)} %copy.221) | copy-start | bytes 1572868
  104.0 6.7 %slice-start = ((s8[6291456]{0:T(1024)(128)(4,1)}), s8[4194304]{0:T(1024)(128)(4,1)S(1)}, s32[]{:S(2)}) async-start(s8[6291456]{0:T(1024)(128)(4,1)} %bitcast.179), calls=%async_computation.8 | async-start | bytes 8388608
  109.7 4.1 %slice-start.2 = ((s8[6291456]{0:T(1024)(128)(4,1)}), s8[4194304]{0:T(1024)(128)(4,1)S(1)}, s32[]{:S(2)}) async-start(s8[6291456]{0:T(1024)(128)(4,1)} %bitcast.181), calls=%async_computation.10 | async-start | bytes 8388608
  110.8 3.1 %slice-start.3 = ((s8[6291456]{0:T(1024)(128)(4,1)}), s8[2097152]{0:T(1024)(128)(4,1)S(1)}, s32[]{:S(2)}) async-start(s8[6291456]{0:T(1024)(128)(4,1)} %bitcast.181), calls=%async_computation.11 | async-start | bytes 4194304
  113.8 2.9 %copy-start.13 = (bf16[512,1,1,512]{0,3,2,1:T(8,128)(2,1)S(1)}, bf16[512,1,1,512]{0,3,2,1:T(8,128)(2,1)}, u32[]{:S(2)}) copy-start(bf16[512,1,1,512]{0,3,2,1:T(8,128)(2,1)} %copy.172) | copy-start | bytes 1572868
  118.6 3.0 %copy-start = (f32[2,1536,1,256]{3,1,0,2:T(8,128)}, f32[2,1536,1,256]{3,1,0,2:T(8,128)S(1)}, u32[]{:S(2)}) copy-start(f32[2,1536,1,256]{3,1,0,2:T(8,128)S(1)} %get-tuple-element.21) | copy-start | bytes 9437188
  121.6 55.2 %collective-permute-start.2 = (f32[2,512,2,256]{3,1,0,2:T(8,128)}, f32[2,512,2,256]{3,1,0,2:T(8,128)}, u32[]{:S(2)}, u32[]{:S(2)}) collective-permute-start(f32[2,512,2,256]{3,1,0,2:T(8,128)} %get-tuple-element.4), channel_id=1, source_target_pairs={{4,0},{8,4},{12,8},{16,12},{20,16},{24,20},{28,24},{32,28},{36,32}... | collective-permute-start | bytes 6291464 | tf_op jit(solution)/shard_map/ppermute | solution.py:16
  132.0 74.4 %collective-permute-start.3 = (f32[2,512,2,256]{3,1,0,2:T(8,128)}, f32[2,512,2,256]{3,1,0,2:T(8,128)}, u32[]{:S(2)}, u32[]{:S(2)}) collective-permute-start(f32[2,512,2,256]{3,1,0,2:T(8,128)} %get-tuple-element.5), channel_id=1, source_target_pairs={{8,0},{12,4},{16,8},{20,12},{24,16},{28,20},{32,24},{36,28},{40,32... | collective-permute-start | bytes 6291464 | tf_op jit(solution)/shard_map/ppermute | solution.py:16
  145.7 24.0 %all-to-all-start.3 = ((bf16[512,1,2,512]{3,2,1,0:T(2,128)(2,1)}), bf16[512,1,2,512]{3,2,1,0:T(2,128)(2,1)}, u32[]{:S(2)}, u32[]{:S(2)}) async-start(bf16[512,1,2,512]{3,2,1,0:T(2,128)(2,1)} %pad_maximum_fusion.2), calls=%async_computation.3 | async-start | bytes 2097152 | tf_op jit(solution)/shard_map/all_to_all | solution.py:137
  169.7 41.0 %all-to-all-start.5 = ((bf16[512,1,2,512]{3,2,1,0:T(2,128)(2,1)}), bf16[512,1,2,512]{3,2,1,0:T(2,128)(2,1)}, u32[]{:S(2)}, u32[]{:S(2)}) async-start(bf16[512,1,2,512]{3,2,1,0:T(2,128)(2,1)} %pad_maximum_fusion.3), calls=%async_computation.5 | async-start | bytes 2097152 | tf_op jit(solution)/shard_map/all_to_all | solution.py:138
  210.7 11.4 %all-to-all-start.7 = ((bf16[512,1,2,256]{3,2,1,0:T(2,128)(2,1)}), bf16[512,1,2,256]{3,2,1,0:T(2,128)(2,1)S(1)}, u32[]{:S(2)}, u32[]{:S(2)}) async-start(bf16[512,1,2,256]{3,2,1,0:T(2,128)(2,1)} %copy.198), calls=%async_computation.7 | async-start | bytes 1048576 | tf_op jit(solution)/shard_map/all_to_all | solution.py:140
  222.1 13.6 %all-to-all-start.6 = ((bf16[512,1,2,256]{3,2,1,0:T(2,128)(2,1)}), bf16[512,1,2,256]{3,2,1,0:T(2,128)(2,1)S(1)}, u32[]{:S(2)}, u32[]{:S(2)}) async-start(bf16[512,1,2,256]{3,2,1,0:T(2,128)(2,1)} %copy.196), calls=%async_computation.6 | async-start | bytes 1048576 | tf_op jit(solution)/shard_map/all_to_all | solution.py:139
  (6 other events, 10.0 us)
where the time goes:
time: 239 us; the launch traced here: 237 us
  waiting for transfers between devices  66.4 us (28%)
  starting transfers between devices  58.5 us (24%)
  local copies, waits for them, and re-layouts  51.2 us (21%)
  matrix products  32.6 us (14%)
  other arithmetic  27.6 us (12%)
    ppermute x4, waiting for transfers between devices, passed_along(): return lax.ppermute(block, axis, route)  43.1 us
    ppermute x4, starting transfers between devices, passed_along(): return lax.ppermute(block, axis, route)  19.4 us
    sub x2, matrix products, tile_pass(): weights = jnp.exp(scores - row_max)  13.6 us
    unnamed x54, local copies, waits for them, and re-layouts  12.5 us
    dot_general x2, matrix products, tile_pass(): jnp.einsum('gqk,kd->qgd', grad_low, key_block, preferred_element_type=jnp...  7.86 us
    convert_element_type x2, other arithmetic, tile_pass(): probs_low = probs_full.astype(jnp.bfloat16)  7.57 us
    another operation x2, local copies, waits for them, and re-layouts, attend(): jnp.stack([swept_head[0] for swept_head in outputs], axis=1)  7.13 us
    another operation x2, local copies, waits for them, and re-layouts, attend(): jnp.stack([swept_head[1] for swept_head in outputs], axis=1)  7.12 us
  transfers between devices with their start and end apart: 12, of which 8 were waited for; matrix products, arithmetic and copies ran while one was open for 28% of the time, Pallas kernels for 0%

commit v1 on v0

v1 whole, which is shorter than its diff:
```python
import functools
import math

import jax
import jax.numpy as jnp
from jax import lax
from jax.experimental import pallas as pl
from jax.experimental.pallas import tpu as pltpu
from jax.sharding import PartitionSpec as P

MESH = pl.DeviceIdType.MESH
HEAD_WIDTH = 256
WINDOW = 1024
TILE = 256
SPAN = WINDOW + TILE
SCALE = HEAD_WIDTH ** -0.5
LOG2E = math.log2(math.e)
HIDDEN = -1e30
NT = (((1,), (1,)), ((), ()))
NN = (((1,), (0,)), ((), ()))
TN = (((0,), (0,)), ((), ()))


def dot(left, right, dims):
    return lax.dot_general(left, right, dims, preferred_element_type=jnp.float32)


def kernel(
    chips,
    block,
    group,
    q_hbm,
    k_hbm,
    v_hbm,
    g_hbm,
    lens,
    o_hbm,
    dq_hbm,
    dk_hbm,
    dv_hbm,
    q_own,
    g_own,
    k_win,
    v_win,
    o_own,
    dq_own,
    probs,
    first_key,
    dk_sum,
    dv_sum,
    rim_dk,
    rim_dv,
    back_dk,
    back_dv,
    dk_own,
    dv_own,
    in_send,
    in_recv,
    rim_send,
    rim_recv,
    back_send,
    back_recv,
    out_send,
    out_recv,
):
    blocks = 2 * chips
    rows = blocks * block
    tiles = rows // TILE
    per_tile = TILE // block
    wide = group * HEAD_WIDTH
    seq = lax.axis_index("seq")
    x = lax.axis_index("head")
    seqs = lax.axis_size("seq")
    core = lax.rem(seq, 2)
    row_base = seq - core
    mine = core * chips + x
    head = 2 * x + core
    after = (lax.rem(seq + 2, seqs), x)
    before = (lax.rem(seq + seqs - 2, seqs), x)

    peers = []
    for dx, dc in ((0, 1), (1, 0), (chips - 1, 0), (1, 1), (chips - 1, 1), (2, 0), (2, 1)):
        peer_core = lax.rem(core + dc, 2)
        peer_x = lax.rem(x + dx, chips)
        peers.append((row_base + peer_core, peer_x, peer_core * chips + peer_x, 2 * peer_x + peer_core))

    barrier = pltpu.get_barrier_semaphore()
    for peer in peers:
        pl.semaphore_signal(barrier, inc=1, device_id=(peer[0], peer[1]), device_id_type=MESH)
    pl.semaphore_signal(barrier, inc=1, device_id=after, device_id_type=MESH)
    pl.semaphore_signal(barrier, inc=1, device_id=before, device_id_type=MESH)

    def block_rows(index, offset=0):
        return pl.ds(pl.multiple_of(offset + index * block, block), block)

    def head_columns(index, width):
        return pl.ds(pl.multiple_of(index * width, width), width)

    moves = (
        (k_hbm, k_win, HEAD_WIDTH, WINDOW),
        (v_hbm, v_win, HEAD_WIDTH, WINDOW),
        (q_hbm, q_own, wide, 0),
        (g_hbm, g_own, wide, 0),
    )
    for a, (source, target, width, offset) in enumerate(moves):
        pltpu.make_async_copy(
            source.at[:, head_columns(head, width)],
            target.at[block_rows(mine, offset), :],
            in_recv.at[a, mine],
        ).start()

    place = (seq // 2) * rows + lax.broadcasted_iota(jnp.int32, (8, rows), 1)

    def next_doc(d, carry):
        start, first = carry
        return start + lens[d], jnp.where(place >= start, start, first)

    _, first = lax.fori_loop(
        0, lens.shape[0], next_doc, (jnp.int32(0), jnp.zeros((8, rows), jnp.int32))
    )
    in_row = lax.broadcasted_iota(jnp.int32, (8, rows), 1)
    tile_start = in_row // TILE * TILE
    first = jnp.maximum(first, place - (WINDOW - 1)) - (place - in_row - WINDOW) - tile_start
    first_key[...] = jnp.transpose(jnp.concatenate([first] * 16, axis=0))
    dk_sum[...] = jnp.zeros_like(dk_sum)
    dv_sum[...] = jnp.zeros_like(dv_sum)

    pl.semaphore_wait(barrier, len(peers) + 2)

    sends = []
    for a, (source, target, width, offset) in enumerate(moves):
        for n, peer in enumerate(peers):
            copy = pltpu.make_async_remote_copy(
                src_ref=source.at[:, head_columns(peer[3], width)],
                dst_ref=target.at[block_rows(mine, offset), :],
                send_sem=in_send.at[a, n],
                recv_sem=in_recv.at[a, mine],
                device_id=(peer[0], peer[1]),
                device_id_type=MESH,
            )
            copy.start()
            sends.append(copy)

    def arrived(a, index):
        source, target, width, offset = moves[a]
        landed = target.at[block_rows(index, offset), :]
        pltpu.make_async_copy(landed, landed, in_recv.at[a, index]).wait()

    for index in [mine] + [peer[2] for peer in peers]:
        for a, window in ((0, k_win), (1, v_win)):
            arrived(a, index)
            copy = pltpu.make_async_remote_copy(
                src_ref=window.at[block_rows(index, WINDOW), :],
                dst_ref=window.at[block_rows(index), :],
                send_sem=rim_send.at[a, index],
                recv_sem=rim_recv.at[a, index],
                device_id=after,
                device_id_type=MESH,
            )
            copy.start()
            sends.append(copy)

    for index in range(blocks):
        arrived(2, index)
    for index in range(blocks):
        for a, window in ((0, k_win), (1, v_win)):
            landed = window.at[block_rows(index), :]
            pltpu.make_async_copy(landed, landed, rim_recv.at[a, index]).wait()

    def send_home(a, source, target, width, index):
        owner = (row_base + index // chips, lax.rem(index, chips))

        @pl.when(index == mine)
        def _():
            pltpu.make_async_copy(
                source.at[block_rows(index), :],
                target.at[:, head_columns(head, width)],
                out_recv.at[a, head],
            ).start()

        @pl.when(index != mine)
        def _():
            pltpu.make_async_remote_copy(
                src_ref=source.at[block_rows(index), :],
                dst_ref=target.at[:, head_columns(head, width)],
                send_sem=out_send.at[a, index],
                recv_sem=out_recv.at[a, head],
                device_id=owner,
                device_id_type=MESH,
            ).start()

    column = lax.broadcasted_iota(jnp.int32, (TILE, SPAN), 1)
    last_key = lax.broadcasted_iota(jnp.int32, (TILE, SPAN), 0) + WINDOW

    @pl.loop(0, tiles)
    def _(t):
        at = pl.multiple_of(t * TILE, TILE)
        keys = pl.ds(at, SPAN)
        for g in range(group):
            columns = slice(g * HEAD_WIDTH, (g + 1) * HEAD_WIDTH)
            scores = dot(q_own[pl.ds(at, TILE), columns], k_win[keys, :], NT)
            visible = (column >= first_key[pl.ds(at, TILE), 0:1]) & (column <= last_key)
            scores = jnp.where(visible, scores, HIDDEN)
            top = jnp.max(scores, axis=1, keepdims=True)
            weights = jnp.exp2((scores - top) * (SCALE * LOG2E))
            total = jnp.sum(weights, axis=1, keepdims=True)
            probs_low = (weights * (1.0 / total)).astype(jnp.bfloat16)
            probs[t, g * TILE : (g + 1) * TILE, :] = probs_low
            o_own[pl.ds(at, TILE), columns] = dot(probs_low, v_win[keys, :], NN).astype(jnp.bfloat16)
        for n in range(per_tile):
            send_home(0, o_own, o_hbm, wide, t * per_tile + n)

    for index in range(blocks):
        arrived(3, index)

    def summed(sums, chunk_start, scale):
        chunk = jnp.transpose(sums[:, pl.ds(chunk_start, TILE)])
        return chunk * scale if scale is not None else chunk

    @pl.loop(0, tiles)
    def _(t):
        at = pl.multiple_of(t * TILE, TILE)
        keys = pl.ds(at, SPAN)
        for g in range(group):
            columns = slice(g * HEAD_WIDTH, (g + 1) * HEAD_WIDTH)
            query = q_own[pl.ds(at, TILE), columns]
            grad = g_own[pl.ds(at, TILE), columns]
            low = o_own[pl.ds(at, TILE), columns]
            delta = jnp.sum(grad.astype(jnp.float32) * low.astype(jnp.float32), axis=1, keepdims=True)
            probs_low = probs[t, g * TILE : (g + 1) * TILE, :]
            dv_sum[:, keys] += dot(grad, probs_low, TN)
            grad_probs = dot(grad, v_win[keys, :], NT)
            grad_low = (probs_low.astype(jnp.float32) * (grad_probs - delta)).astype(jnp.bfloat16)
            dq_own[pl.ds(at, TILE), columns] = (dot(grad_low, k_win[keys, :], NN) * SCALE).astype(
                jnp.bfloat16
            )
            dk_sum[:, keys] += dot(query, grad_low, TN)
        for n in range(per_tile):
            send_home(1, dq_own, dq_hbm, wide, t * per_tile + n)
        for a, sums, rim, back, scale in (
            (0, dk_sum, rim_dk, back_dk, SCALE),
            (1, dv_sum, rim_dv, back_dv, None),
        ):
            rim[pl.ds(at, TILE), :] = summed(sums, at, scale).astype(jnp.bfloat16)
            pltpu.make_async_remote_copy(
                src_ref=rim.at[pl.ds(at, TILE), :],
                dst_ref=back.at[pl.ds(at, TILE), :],
                send_sem=back_send.at[a, t],
                recv_sem=back_recv.at[a, t],
                device_id=before,
                device_id_type=MESH,
            ).start()

    @pl.loop(0, tiles)
    def _(t):
        at = pl.multiple_of(t * TILE, TILE)
        for a, sums, back, own, target, scale in (
            (0, dk_sum, back_dk, dk_own, dk_hbm, SCALE),
            (1, dv_sum, back_dv, dv_own, dv_hbm, None),
        ):
            landed = back.at[pl.ds(at, TILE), :]
            pltpu.make_async_copy(landed, landed, back_recv.at[a, t]).wait()
            total = summed(sums, WINDOW + at, scale) + back[pl.ds(at, TILE), :].astype(jnp.float32)
            own[pl.ds(at, TILE), :] = total.astype(jnp.bfloat16)
            for n in range(per_tile):
                send_home(2 + a, own, target, HEAD_WIDTH, t * per_tile + n)

    for copy in sends:
        copy.wait_send()
    results = (
        (o_own, o_hbm, wide),
        (dq_own, dq_hbm, wide),
        (dk_own, dk_hbm, HEAD_WIDTH),
        (dv_own, dv_hbm, HEAD_WIDTH),
    )
    for a, rim in ((0, rim_dk), (1, rim_dv)):
        for t in range(tiles):
            sent = rim.at[pl.ds(t * TILE, TILE), :]
            pltpu.make_async_copy(sent, sent, back_send.at[a, t]).wait()
    for a, (source, target, width) in enumerate(results):
        for index in range(blocks):

            @pl.when(index != mine)
            def _():
                sent = source.at[block_rows(index), :]
                pltpu.make_async_copy(sent, sent, out_send.at[a, index]).wait()

        for h in range(blocks):
            landed = target.at[:, h * width : (h + 1) * width]
            pltpu.make_async_copy(landed, landed, out_recv.at[a, h]).wait()


def shards(rotated_query_rows, rotated_key_rows, value_matrix, output_gradient, doc_lengths):
    chips = lax.axis_size("head")
    block, query_columns = rotated_query_rows.shape
    key_columns = rotated_key_rows.shape[1]
    group = query_columns // key_columns
    blocks = 2 * chips
    rows = blocks * block
    tiles = rows // TILE
    wide = group * HEAD_WIDTH
    low = jnp.bfloat16
    hbm = pl.BlockSpec(memory_space=pl.ANY)
    return pl.pallas_call(
        functools.partial(kernel, chips, block, group),
        out_shape=(
            jax.ShapeDtypeStruct((block, query_columns), low),
            jax.ShapeDtypeStruct((block, query_columns), low),
            jax.ShapeDtypeStruct((block, key_columns), low),
            jax.ShapeDtypeStruct((block, key_columns), low),
        ),
        in_specs=[hbm] * 4 + [pl.BlockSpec(memory_space=pltpu.SMEM)],
        out_specs=(hbm,) * 4,
        scratch_shapes=[
            pltpu.VMEM((rows, wide), low),
            pltpu.VMEM((rows, wide), low),
            pltpu.VMEM((WINDOW + rows, HEAD_WIDTH), low),
            pltpu.VMEM((WINDOW + rows, HEAD_WIDTH), low),
            pltpu.VMEM((rows, wide), low),
            pltpu.VMEM((rows, wide), low),
            pltpu.VMEM((tiles, group * TILE, SPAN), low),
            pltpu.VMEM((rows, 128), jnp.int32),
            pltpu.VMEM((HEAD_WIDTH, WINDOW + rows), jnp.float32),
            pltpu.VMEM((HEAD_WIDTH, WINDOW + rows), jnp.float32),
            pltpu.VMEM((rows, HEAD_WIDTH), low),
            pltpu.VMEM((rows, HEAD_WIDTH), low),
            pltpu.VMEM((rows, HEAD_WIDTH), low),
            pltpu.VMEM((rows, HEAD_WIDTH), low),
            pltpu.VMEM((rows, HEAD_WIDTH), low),
            pltpu.VMEM((rows, HEAD_WIDTH), low),
            pltpu.SemaphoreType.DMA((4, blocks - 1)),
            pltpu.SemaphoreType.DMA((4, blocks)),
            pltpu.SemaphoreType.DMA((2, blocks)),
            pltpu.SemaphoreType.DMA((2, blocks)),
            pltpu.SemaphoreType.DMA((2, tiles)),
            pltpu.SemaphoreType.DMA((2, tiles)),
            pltpu.SemaphoreType.DMA((4, blocks)),
            pltpu.SemaphoreType.DMA((4, blocks)),
        ],
        compiler_params=pltpu.CompilerParams(
            collective_id=0, has_side_effects=True, vmem_limit_bytes=48 * 2**20
        ),
    )(rotated_query_rows, rotated_key_rows, value_matrix, output_gradient, doc_lengths)


def solution(mesh):
    rows = P(("seq", "head"), None)
    return jax.shard_map(
        shards,
        mesh=mesh,
        in_specs=(rows, rows, rows, rows, P()),
        out_specs=(rows, rows, rows, rows),
        check_vma=False,
    )
```

time: 239 us -> 90.3 us (0.38)
  the two profiles are of different devices: /device:TPU:122 before, /device:TPU:1 now
where the time goes in v1:
time: 90.3 us; the launch traced here: 90 us
  Pallas kernels  81.9 us (91%)
  local copies, waits for them, and re-layouts  7.48 us (8%)
    pallas_call x1, Pallas kernels, shards(): pl.pallas_call(functools.partial(kernel, chips, block, group), out_shape=...  81.9 us
    unnamed x12, local copies, waits for them, and re-layouts  7.48 us

profile of v1, /device:TPU:1, one launch (start us, length us, event | category | flops | bytes accessed | tf_op | source)
XLA Modules:
  0.0 90.0 jit_solution(17476356858318607426)
XLA Ops:
  0.6 0.0 copy-start
  0.6 1.2 %copy-done = bf16[128,4096]{1,0:T(8,128)(2,1)S(1)} copy-done((bf16[128,4096]{1,0:T(8,128)(2,1)S(1)}, bf16[128,4096]{1,0:T(8,128)(2,1)}, u32[]{:S(2)}) %copy-start) | copy-done | bytes 1048600
  1.9 0.0 copy-start.1
  1.9 1.0 %copy-done.1 = bf16[128,2048]{1,0:T(8,128)(2,1)S(1)} copy-done((bf16[128,2048]{1,0:T(8,128)(2,1)S(1)}, bf16[128,2048]{1,0:T(8,128)(2,1)}, u32[]{:S(2)}) %copy-start.1) | copy-done | bytes 524312
  2.9 0.0 copy-start.2
  2.9 1.0 %copy-done.2 = bf16[128,2048]{1,0:T(8,128)(2,1)S(1)} copy-done((bf16[128,2048]{1,0:T(8,128)(2,1)S(1)}, bf16[128,2048]{1,0:T(8,128)(2,1)}, u32[]{:S(2)}) %copy-start.2) | copy-done | bytes 524312
  3.9 0.0 copy-start.3
  3.9 0.7 copy-done.3
  4.6 81.9 %shard_map.84 = (bf16[128,4096]{1,0:T(8,128)(2,1)S(1)}, bf16[128,4096]{1,0:T(8,128)(2,1)S(1)}, bf16[128,2048]{1,0:T(8,128)(2,1)S(1)}, bf16[128,2048]{1,0:T(8,128)(2,1)S(1)}) custom-call(bf16[128,4096]{1,0:T(8,128)(2,1)S(1)} %copy-done, bf16[128,2048]{1,0:T(8,128)(2,1)S(1)} %copy-done.1, bf16[128,2048]{1,0:T(8,128)(2,1)S(1)} %copy-done.2, ...), custom_call_target="tpu_custom_call" | custom-call | tf_op jit(solution)/shard_map/pallas_call | solution.py:304
  86.5 1.0 %copy.13 = bf16[128,4096]{1,0:T(8,128)(2,1)} copy(bf16[128,4096]{1,0:T(8,128)(2,1)S(1)} %get-tuple-element.8) | data formatting | bytes 2097152
  87.5 1.0 %copy.14 = bf16[128,4096]{1,0:T(8,128)(2,1)} copy(bf16[128,4096]{1,0:T(8,128)(2,1)S(1)} %get-tuple-element.9) | data formatting | bytes 2097152
  88.5 0.8 copy.15
  89.3 0.8 copy.16
Async XLA Ops:
  0.6 1.2 %copy-start = (bf16[128,4096]{1,0:T(8,128)(2,1)S(1)}, bf16[128,4096]{1,0:T(8,128)(2,1)}, u32[]{:S(2)}) copy-start(bf16[128,4096]{1,0:T(8,128)(2,1)} %q_hbm.1) | copy-start | bytes 3145732
  1.9 1.0 %copy-start.1 = (bf16[128,2048]{1,0:T(8,128)(2,1)S(1)}, bf16[128,2048]{1,0:T(8,128)(2,1)}, u32[]{:S(2)}) copy-start(bf16[128,2048]{1,0:T(8,128)(2,1)} %k_hbm.1) | copy-start | bytes 1572868
  2.9 1.0 %copy-start.2 = (bf16[128,2048]{1,0:T(8,128)(2,1)S(1)}, bf16[128,2048]{1,0:T(8,128)(2,1)}, u32[]{:S(2)}) copy-start(bf16[128,2048]{1,0:T(8,128)(2,1)} %v_hbm.1) | copy-start | bytes 1572868
  3.9 0.7 copy-start.3

commit v2 on v1

--- a/solution.py
+++ b/solution.py
@@ -77,6 +77,8 @@
     head = 2 * x + core
     after = (lax.rem(seq + 2, seqs), x)
     before = (lax.rem(seq + seqs - 2, seqs), x)
+    has_after = seq + 2 < seqs
+    has_before = seq >= 2
 
     peers = []
     for dx, dc in ((0, 1), (1, 0), (chips - 1, 0), (1, 1), (chips - 1, 1), (2, 0), (2, 1)):
@@ -87,8 +89,14 @@
     barrier = pltpu.get_barrier_semaphore()
     for peer in peers:
         pl.semaphore_signal(barrier, inc=1, device_id=(peer[0], peer[1]), device_id_type=MESH)
-    pl.semaphore_signal(barrier, inc=1, device_id=after, device_id_type=MESH)
-    pl.semaphore_signal(barrier, inc=1, device_id=before, device_id_type=MESH)
+
+    @pl.when(has_after)
+    def _():
+        pl.semaphore_signal(barrier, inc=1, device_id=after, device_id_type=MESH)
+
+    @pl.when(has_before)
+    def _():
+        pl.semaphore_signal(barrier, inc=1, device_id=before, device_id_type=MESH)
 
     def block_rows(index, offset=0):
         return pl.ds(pl.multiple_of(offset + index * block, block), block)
@@ -125,7 +133,17 @@
     dk_sum[...] = jnp.zeros_like(dk_sum)
     dv_sum[...] = jnp.zeros_like(dv_sum)
 
-    pl.semaphore_wait(barrier, len(peers) + 2)
+    @pl.when(jnp.logical_not(has_before))
+    def _():
+        k_win[0:WINDOW, :] = jnp.zeros((WINDOW, HEAD_WIDTH), k_win.dtype)
+        v_win[0:WINDOW, :] = jnp.zeros((WINDOW, HEAD_WIDTH), v_win.dtype)
+
+    @pl.when(jnp.logical_not(has_after))
+    def _():
+        back_dk[...] = jnp.zeros_like(back_dk)
+        back_dv[...] = jnp.zeros_like(back_dv)
+
+    pl.semaphore_wait(barrier, len(peers) + has_after.astype(jnp.int32) + has_before.astype(jnp.int32))
 
     sends = []
     for a, (source, target, width, offset) in enumerate(moves):
@@ -149,23 +167,27 @@
     for index in [mine] + [peer[2] for peer in peers]:
         for a, window in ((0, k_win), (1, v_win)):
             arrived(a, index)
-            copy = pltpu.make_async_remote_copy(
-                src_ref=window.at[block_rows(index, WINDOW), :],
-                dst_ref=window.at[block_rows(index), :],
-                send_sem=rim_send.at[a, index],
-                recv_sem=rim_recv.at[a, index],
-                device_id=after,
-                device_id_type=MESH,
-            )
-            copy.start()
-            sends.append(copy)
+
+            @pl.when(has_after)
+            def _():
+                pltpu.make_async_remote_copy(
+                    src_ref=window.at[block_rows(index, WINDOW), :],
+                    dst_ref=window.at[block_rows(index), :],
+                    send_sem=rim_send.at[a, index],
+                    recv_sem=rim_recv.at[a, index],
+                    device_id=after,
+                    device_id_type=MESH,
+                ).start()
 
     for index in range(blocks):
         arrived(2, index)
-    for index in range(blocks):
-        for a, window in ((0, k_win), (1, v_win)):
-            landed = window.at[block_rows(index), :]
-            pltpu.make_async_copy(landed, landed, rim_recv.at[a, index]).wait()
+
+    @pl.when(has_before)
+    def _():
+        for index in range(blocks):
+            for a, window in ((0, k_win), (1, v_win)):
+                landed = window.at[block_rows(index), :]
+                pltpu.make_async_copy(landed, landed, rim_recv.at[a, index]).wait()
 
     def send_home(a, source, target, width, index):
         owner = (row_base + index // chips, lax.rem(index, chips))
@@ -242,14 +264,17 @@
             (1, dv_sum, rim_dv, back_dv, None),
         ):
             rim[pl.ds(at, TILE), :] = summed(sums, at, scale).astype(jnp.bfloat16)
-            pltpu.make_async_remote_copy(
-                src_ref=rim.at[pl.ds(at, TILE), :],
-                dst_ref=back.at[pl.ds(at, TILE), :],
-                send_sem=back_send.at[a, t],
-                recv_sem=back_recv.at[a, t],
-                device_id=before,
-                device_id_type=MESH,
-            ).start()
+
+            @pl.when(has_before)
+            def _():
+                pltpu.make_async_remote_copy(
+                    src_ref=rim.at[pl.ds(at, TILE), :],
+                    dst_ref=back.at[pl.ds(at, TILE), :],
+                    send_sem=back_send.at[a, t],
+                    recv_sem=back_recv.at[a, t],
+                    device_id=before,
+                    device_id_type=MESH,
+                ).start()
 
     @pl.loop(0, tiles)
     def _(t):
@@ -258,8 +283,12 @@
             (0, dk_sum, back_dk, dk_own, dk_hbm, SCALE),
             (1, dv_sum, back_dv, dv_own, dv_hbm, None),
         ):
-            landed = back.at[pl.ds(at, TILE), :]
-            pltpu.make_async_copy(landed, landed, back_recv.at[a, t]).wait()
+
+            @pl.when(has_after)
+            def _():
+                landed = back.at[pl.ds(at, TILE), :]
+                pltpu.make_async_copy(landed, landed, back_recv.at[a, t]).wait()
+
             total = summed(sums, WINDOW + at, scale) + back[pl.ds(at, TILE), :].astype(jnp.float32)
             own[pl.ds(at, TILE), :] = total.astype(jnp.bfloat16)
             for n in range(per_tile):
@@ -273,10 +302,21 @@
         (dk_own, dk_hbm, HEAD_WIDTH),
         (dv_own, dv_hbm, HEAD_WIDTH),
     )
-    for a, rim in ((0, rim_dk), (1, rim_dv)):
-        for t in range(tiles):
-            sent = rim.at[pl.ds(t * TILE, TILE), :]
-            pltpu.make_async_copy(sent, sent, back_send.at[a, t]).wait()
+
+    @pl.when(has_after)
+    def _():
+        for a, window in ((0, k_win), (1, v_win)):
+            for index in range(blocks):
+                sent = window.at[block_rows(index, WINDOW), :]
+                pltpu.make_async_copy(sent, sent, rim_send.at[a, index]).wait()
+
+    @pl.when(has_before)
+    def _():
+        for a, rim in ((0, rim_dk), (1, rim_dv)):
+            for t in range(tiles):
+                sent = rim.at[pl.ds(t * TILE, TILE), :]
+                pltpu.make_async_copy(sent, sent, back_send.at[a, t]).wait()
+
     for a, (source, target, width) in enumerate(results):
         for index in range(blocks):
 
@@ -288,6 +328,18 @@
         for h in range(blocks):
             landed = target.at[:, h * width : (h + 1) * width]
             pltpu.make_async_copy(landed, landed, out_recv.at[a, h]).wait()
+
+
+def land(*refs):
+    half = len(refs) // 2
+    sems = refs[-1]
+    copies = [
+        pltpu.make_async_copy(refs[n], refs[half + n], sems.at[n]) for n in range(half)
+    ]
+    for copy in copies:
+        copy.start()
+    for copy in copies:
+        copy.wait()
 
 
 def shards(rotated_query_rows, rotated_key_rows, value_matrix, output_gradient, doc_lengths):
@@ -301,14 +353,15 @@
     wide = group * HEAD_WIDTH
     low = jnp.bfloat16
     hbm = pl.BlockSpec(memory_space=pl.ANY)
-    return pl.pallas_call(
+    shapes = (
+        jax.ShapeDtypeStruct((block, query_columns), low),
+        jax.ShapeDtypeStruct((block, query_columns), low),
+        jax.ShapeDtypeStruct((block, key_columns), low),
+        jax.ShapeDtypeStruct((block, key_columns), low),
+    )
+    results = pl.pallas_call(
         functools.partial(kernel, chips, block, group),
-        out_shape=(
-            jax.ShapeDtypeStruct((block, query_columns), low),
-            jax.ShapeDtypeStruct((block, query_columns), low),
-            jax.ShapeDtypeStruct((block, key_columns), low),
-            jax.ShapeDtypeStruct((block, key_columns), low),
-        ),
+        out_shape=shapes,
         in_specs=[hbm] * 4 + [pl.BlockSpec(memory_space=pltpu.SMEM)],
         out_specs=(hbm,) * 4,
         scratch_shapes=[
@@ -340,7 +393,26 @@
         compiler_params=pltpu.CompilerParams(
             collective_id=0, has_side_effects=True, vmem_limit_bytes=48 * 2**20
         ),
-    )(rotated_query_rows, rotated_key_rows, value_matrix, output_gradient, doc_lengths)
+    )(
+        *(
+            pltpu.with_memory_space_constraint(array, pltpu.HBM)
+            for array in (
+                rotated_query_rows,
+                rotated_key_rows,
+                value_matrix,
+                output_gradient,
+                doc_lengths,
+            )
+        )
+    )
+    return pl.pallas_call(
+        land,
+        out_shape=tuple(pltpu.HBM(shape.shape, shape.dtype) for shape in shapes),
+        in_specs=[hbm] * len(shapes),
+        out_specs=(pl.BlockSpec(memory_space=pltpu.HBM),) * len(shapes),
+        scratch_shapes=[pltpu.SemaphoreType.DMA((len(shapes),))],
+        compiler_params=pltpu.CompilerParams(vmem_limit_bytes=2**20),
+    )(*(pltpu.with_memory_space_constraint(result, pltpu.VMEM) for result in results))
 
 
 def solution(mesh):

time: 90.3 us -> 79.2 us (0.88)
  local copies, waits for them, and re-layouts: 7.48 us -> 0 us
  Pallas kernels: 81.9 us -> 78.5 us
    unnamed x12 -> x0, local copies, waits for them, and re-layouts: 7.48 us -> none
    pallas_call x1, Pallas kernels: 81.9 us -> 76.8 us  [shards(): pl.pallas_call(functools.partial(kernel, chips, block, group), out_shape=...]
    pallas_call x0 -> x1, Pallas kernels: none -> 1.69 us  [shards(): pl.pallas_call(land, out_shape=tuple((pltpu.HBM(shape.shape, shape.dtype)...]
where the time goes in v2:
time: 79.2 us; the launch traced here: 79.1 us
  Pallas kernels  78.5 us (99%)
    pallas_call x1, Pallas kernels, shards(): pl.pallas_call(functools.partial(kernel, chips, block, group), out_shape=...  76.8 us
    pallas_call x1, Pallas kernels, shards(): pl.pallas_call(land, out_shape=tuple((pltpu.HBM(shape.shape, shape.dtype)...  1.69 us

profile of v2, /device:TPU:1, one launch (start us, length us, event | category | flops | bytes accessed | tf_op | source)
XLA Modules:
  0.0 79.1 jit_solution(14489245998802284940)
XLA Ops:
  0.6 76.8 %shard_map.84 = (bf16[128,4096]{1,0:T(8,128)(2,1)S(1)}, bf16[128,4096]{1,0:T(8,128)(2,1)S(1)}, bf16[128,2048]{1,0:T(8,128)(2,1)S(1)}, bf16[128,2048]{1,0:T(8,128)(2,1)S(1)}) custom-call(bf16[128,4096]{1,0:T(8,128)(2,1)} %q_hbm.1, bf16[128,2048]{1,0:T(8,128)(2,1)} %k_hbm.1, bf16[128,2048]{1,0:T(8,128)(2,1)} %v_hbm.1, bf16[128,4096]{1,0:T(8,128)(2,1)} %g_hbm.1, ...), custom_call_target="tpu_custom_call" | custom-call | tf_op jit(solution)/shard_map/pallas_call | solution.py:362
  77.4 1.7 %shard_map.85 = (bf16[128,4096]{1,0:T(8,128)(2,1)}, bf16[128,4096]{1,0:T(8,128)(2,1)}, bf16[128,2048]{1,0:T(8,128)(2,1)}, bf16[128,2048]{1,0:T(8,128)(2,1)}) custom-call(bf16[128,4096]{1,0:T(8,128)(2,1)S(1)} %get-tuple-element.8.refs_0_, bf16[128,4096]{1,0:T(8,128)(2,1)S(1)} %get-tuple-element.9.refs_1_, bf16[128,2048]{1,0:T(8,128)(2,1)S(1)} %get-tuple-element.10.refs_2_, ...), custom_call_target="tpu_custom_call" | custom-call | tf_op jit(solution)/shard_map/pallas_call | solution.py:408

commit v3 on v2

--- a/solution.py
+++ b/solution.py
@@ -38,6 +38,10 @@
     dq_hbm,
     dk_hbm,
     dv_hbm,
+    q_here,
+    k_here,
+    v_here,
+    g_here,
     q_own,
     g_own,
     k_win,
@@ -54,6 +58,7 @@
     back_dv,
     dk_own,
     dv_own,
+    here_sem,
     in_send,
     in_recv,
     rim_send,
@@ -81,7 +86,7 @@
     has_before = seq >= 2
 
     peers = []
-    for dx, dc in ((0, 1), (1, 0), (chips - 1, 0), (1, 1), (chips - 1, 1), (2, 0), (2, 1)):
+    for dx, dc in ((0, 1), (2, 0), (2, 1), (1, 0), (chips - 1, 0), (1, 1), (chips - 1, 1)):
         peer_core = lax.rem(core + dc, 2)
         peer_x = lax.rem(x + dx, chips)
         peers.append((row_base + peer_core, peer_x, peer_core * chips + peer_x, 2 * peer_x + peer_core))
@@ -98,6 +103,10 @@
     def _():
         pl.semaphore_signal(barrier, inc=1, device_id=before, device_id_type=MESH)
 
+    held = ((k_hbm, k_here), (v_hbm, v_here), (q_hbm, q_here), (g_hbm, g_here))
+    for a, (source, target) in enumerate(held):
+        pltpu.make_async_copy(source, target, here_sem.at[a]).start()
+
     def block_rows(index, offset=0):
         return pl.ds(pl.multiple_of(offset + index * block, block), block)
 
@@ -105,43 +114,18 @@
         return pl.ds(pl.multiple_of(index * width, width), width)
 
     moves = (
-        (k_hbm, k_win, HEAD_WIDTH, WINDOW),
-        (v_hbm, v_win, HEAD_WIDTH, WINDOW),
-        (q_hbm, q_own, wide, 0),
-        (g_hbm, g_own, wide, 0),
+        (k_here, k_win, HEAD_WIDTH, WINDOW),
+        (v_here, v_win, HEAD_WIDTH, WINDOW),
+        (q_here, q_own, wide, 0),
+        (g_here, g_own, wide, 0),
     )
     for a, (source, target, width, offset) in enumerate(moves):
+        pltpu.make_async_copy(held[a][0], held[a][1], here_sem.at[a]).wait()
         pltpu.make_async_copy(
             source.at[:, head_columns(head, width)],
             target.at[block_rows(mine, offset), :],
             in_recv.at[a, mine],
         ).start()
-
-    place = (seq // 2) * rows + lax.broadcasted_iota(jnp.int32, (8, rows), 1)
-
-    def next_doc(d, carry):
-        start, first = carry
-        return start + lens[d], jnp.where(place >= start, start, first)
-
-    _, first = lax.fori_loop(
-        0, lens.shape[0], next_doc, (jnp.int32(0), jnp.zeros((8, rows), jnp.int32))
-    )
-    in_row = lax.broadcasted_iota(jnp.int32, (8, rows), 1)
-    tile_start = in_row // TILE * TILE
-    first = jnp.maximum(first, place - (WINDOW - 1)) - (place - in_row - WINDOW) - tile_start
-    first_key[...] = jnp.transpose(jnp.concatenate([first] * 16, axis=0))
-    dk_sum[...] = jnp.zeros_like(dk_sum)
-    dv_sum[...] = jnp.zeros_like(dv_sum)
-
-    @pl.when(jnp.logical_not(has_before))
-    def _():
-        k_win[0:WINDOW, :] = jnp.zeros((WINDOW, HEAD_WIDTH), k_win.dtype)
-        v_win[0:WINDOW, :] = jnp.zeros((WINDOW, HEAD_WIDTH), v_win.dtype)
-
-    @pl.when(jnp.logical_not(has_after))
-    def _():
-        back_dk[...] = jnp.zeros_like(back_dk)
-        back_dv[...] = jnp.zeros_like(back_dv)
 
     pl.semaphore_wait(barrier, len(peers) + has_after.astype(jnp.int32) + has_before.astype(jnp.int32))
 
@@ -178,6 +162,32 @@
                     device_id=after,
                     device_id_type=MESH,
                 ).start()
+
+    place = (seq // 2) * rows + lax.broadcasted_iota(jnp.int32, (8, rows), 1)
+
+    def next_doc(d, carry):
+        start, first = carry
+        return start + lens[d], jnp.where(place >= start, start, first)
+
+    _, first = lax.fori_loop(
+        0, lens.shape[0], next_doc, (jnp.int32(0), jnp.zeros((8, rows), jnp.int32))
+    )
+    in_row = lax.broadcasted_iota(jnp.int32, (8, rows), 1)
+    tile_start = in_row // TILE * TILE
+    first = jnp.maximum(first, place - (WINDOW - 1)) - (place - in_row - WINDOW) - tile_start
+    first_key[...] = jnp.transpose(jnp.concatenate([first] * 16, axis=0))
+    dk_sum[...] = jnp.zeros_like(dk_sum)
+    dv_sum[...] = jnp.zeros_like(dv_sum)
+
+    @pl.when(jnp.logical_not(has_before))
+    def _():
+        k_win[0:WINDOW, :] = jnp.zeros((WINDOW, HEAD_WIDTH), k_win.dtype)
+        v_win[0:WINDOW, :] = jnp.zeros((WINDOW, HEAD_WIDTH), v_win.dtype)
+
+    @pl.when(jnp.logical_not(has_after))
+    def _():
+        back_dk[...] = jnp.zeros_like(back_dk)
+        back_dv[...] = jnp.zeros_like(back_dv)
 
     for index in range(blocks):
         arrived(2, index)
@@ -365,6 +375,10 @@
         in_specs=[hbm] * 4 + [pl.BlockSpec(memory_space=pltpu.SMEM)],
         out_specs=(hbm,) * 4,
         scratch_shapes=[
+            pltpu.VMEM((block, query_columns), low),
+            pltpu.VMEM((block, key_columns), low),
+            pltpu.VMEM((block, key_columns), low),
+            pltpu.VMEM((block, query_columns), low),
             pltpu.VMEM((rows, wide), low),
             pltpu.VMEM((rows, wide), low),
             pltpu.VMEM((WINDOW + rows, HEAD_WIDTH), low),
@@ -381,6 +395,7 @@
             pltpu.VMEM((rows, HEAD_WIDTH), low),
             pltpu.VMEM((rows, HEAD_WIDTH), low),
             pltpu.VMEM((rows, HEAD_WIDTH), low),
+            pltpu.SemaphoreType.DMA((4,)),
             pltpu.SemaphoreType.DMA((4, blocks - 1)),
             pltpu.SemaphoreType.DMA((4, blocks)),
             pltpu.SemaphoreType.DMA((2, blocks)),

time: 79.2 us -> 79.1 us (level)
  no operation moved by 1% of the time
where the time goes in v3:
time: 79.1 us; the launch traced here: 79 us
  Pallas kernels  78.3 us (99%)
    pallas_call x1, Pallas kernels, shards(): pl.pallas_call(functools.partial(kernel, chips, block, group), out_shape=...  76.6 us
    pallas_call x1, Pallas kernels, shards(): pl.pallas_call(land, out_shape=tuple((pltpu.HBM(shape.shape, shape.dtype)...  1.69 us

profile of v3, /device:TPU:1, one launch (start us, length us, event | category | flops | bytes accessed | tf_op | source)
XLA Modules:
  0.0 79.0 jit_solution(3226685257359270140)
XLA Ops:
  0.6 76.6 %shard_map.84 = (bf16[128,4096]{1,0:T(8,128)(2,1)S(1)}, bf16[128,4096]{1,0:T(8,128)(2,1)S(1)}, bf16[128,2048]{1,0:T(8,128)(2,1)S(1)}, bf16[128,2048]{1,0:T(8,128)(2,1)S(1)}) custom-call(bf16[128,4096]{1,0:T(8,128)(2,1)} %q_hbm.1, bf16[128,2048]{1,0:T(8,128)(2,1)} %k_hbm.1, bf16[128,2048]{1,0:T(8,128)(2,1)} %v_hbm.1, bf16[128,4096]{1,0:T(8,128)(2,1)} %g_hbm.1, ...), custom_call_target="tpu_custom_call" | custom-call | tf_op jit(solution)/shard_map/pallas_call | solution.py:372
  77.3 1.7 %shard_map.85 = (bf16[128,4096]{1,0:T(8,128)(2,1)}, bf16[128,4096]{1,0:T(8,128)(2,1)}, bf16[128,2048]{1,0:T(8,128)(2,1)}, bf16[128,2048]{1,0:T(8,128)(2,1)}) custom-call(bf16[128,4096]{1,0:T(8,128)(2,1)S(1)} %get-tuple-element.8.refs_0_, bf16[128,4096]{1,0:T(8,128)(2,1)S(1)} %get-tuple-element.9.refs_1_, bf16[128,2048]{1,0:T(8,128)(2,1)S(1)} %get-tuple-element.10.refs_2_, ...), custom_call_target="tpu_custom_call" | custom-call | tf_op jit(solution)/shard_map/pallas_call | solution.py:423

commit v4 on v3

--- a/solution.py
+++ b/solution.py
@@ -92,7 +92,7 @@
         peers.append((row_base + peer_core, peer_x, peer_core * chips + peer_x, 2 * peer_x + peer_core))
 
     barrier = pltpu.get_barrier_semaphore()
-    for peer in peers:
+    for peer in peers[1:] + peers[:1]:
         pl.semaphore_signal(barrier, inc=1, device_id=(peer[0], peer[1]), device_id_type=MESH)
 
     @pl.when(has_after)
@@ -131,7 +131,7 @@
 
     sends = []
     for a, (source, target, width, offset) in enumerate(moves):
-        for n, peer in enumerate(peers):
+        for n, peer in list(enumerate(peers))[1:] + [(0, peers[0])]:
             copy = pltpu.make_async_remote_copy(
                 src_ref=source.at[:, head_columns(peer[3], width)],
                 dst_ref=target.at[block_rows(mine, offset), :],

time: 79.1 us -> 79.1 us (level)
  no operation moved by 1% of the time
where the time goes in v4:
time: 79.1 us; the launch traced here: 79 us
  Pallas kernels  78.3 us (99%)
    pallas_call x1, Pallas kernels, shards(): pl.pallas_call(functools.partial(kernel, chips, block, group), out_shape=...  76.6 us
    pallas_call x1, Pallas kernels, shards(): pl.pallas_call(land, out_shape=tuple((pltpu.HBM(shape.shape, shape.dtype)...  1.69 us

profile of v4, /device:TPU:1, one launch (start us, length us, event | category | flops | bytes accessed | tf_op | source)
XLA Modules:
  0.0 79.0 jit_solution(3945643274571489222)
XLA Ops:
  0.6 76.6 %shard_map.84 = (bf16[128,4096]{1,0:T(8,128)(2,1)S(1)}, bf16[128,4096]{1,0:T(8,128)(2,1)S(1)}, bf16[128,2048]{1,0:T(8,128)(2,1)S(1)}, bf16[128,2048]{1,0:T(8,128)(2,1)S(1)}) custom-call(bf16[128,4096]{1,0:T(8,128)(2,1)} %q_hbm.1, bf16[128,2048]{1,0:T(8,128)(2,1)} %k_hbm.1, bf16[128,2048]{1,0:T(8,128)(2,1)} %v_hbm.1, bf16[128,4096]{1,0:T(8,128)(2,1)} %g_hbm.1, ...), custom_call_target="tpu_custom_call" | custom-call | tf_op jit(solution)/shard_map/pallas_call | solution.py:372
  77.3 1.7 %shard_map.85 = (bf16[128,4096]{1,0:T(8,128)(2,1)}, bf16[128,4096]{1,0:T(8,128)(2,1)}, bf16[128,2048]{1,0:T(8,128)(2,1)}, bf16[128,2048]{1,0:T(8,128)(2,1)}) custom-call(bf16[128,4096]{1,0:T(8,128)(2,1)S(1)} %get-tuple-element.8.refs_0_, bf16[128,4096]{1,0:T(8,128)(2,1)S(1)} %get-tuple-element.9.refs_1_, bf16[128,2048]{1,0:T(8,128)(2,1)S(1)} %get-tuple-element.10.refs_2_, ...), custom_call_target="tpu_custom_call" | custom-call | tf_op jit(solution)/shard_map/pallas_call | solution.py:423
